TPU v7x, 512 devices: a whole 4x8x8 slice. The times are simulated.
512 devices in a mesh: gx: 64 (over z, x, core), gy: 8 (over y).
Axes of the slice: x: 4, y: 8, z: 8, core: 2. Of those that a mesh axis runs over, the one named last changes fastest.
Arguments:
- velocity: float32 [3, 128, 1536, 128], P(None, 'gx', 'gy'), may hold values from -0.8 to 2.3
- stiffness: float32 [8], P('gy'), may hold values from 100 to 100000
- block_inverse: float32 [3, 1536, 192], P(None, 'gy'), as said below
Outputs:
- velocity_next: float32 [3, 128, 1536, 128], P(None, 'gx', 'gy')
Inputs may be any that keep to these rules, and one draw needn't show every extreme that they name: block_inverse[s] for block k is, to float32 rounding, the inverse of the 192-row matrix with 1 + 2 b on its diagonal and -b beside it, b = alpha_s stiffness[k].
All inputs are finite; a program needn't handle non-finite values.
Results may differ from a plain program's by a relative error of at most 0.0003.
Values sent between devices are 32-bit elements; how exact they have to be, the bound alone decides.
No kernel may reach another device: no remote copies, remote signals or barrier semaphores. Data moves between devices by JAX's collectives and lax.ppermute only.
A program may use at most 64 MiB of HBM per device.

v0:
```python
import jax
import jax.numpy as jnp
from jax import lax
from jax.sharding import PartitionSpec as P

SUBSTEPS = 3
implicit_share = (8.0 / 15.0, 2.0 / 15.0, 1.0 / 3.0)
new_weight = (8.0 / 15.0, 5.0 / 12.0, 3.0 / 4.0)
old_weight = (0.0, -17.0 / 60.0, -5.0 / 12.0)
courant = (0.3, 0.2, 0.3)


def with_halo(cells, sides, width, closed):
    for axis, dim in sides:
        count = lax.axis_size(axis)
        ends = count if closed else count - 1
        head = lax.slice_in_dim(cells, 0, width, axis=dim)
        tail = lax.slice_in_dim(cells, cells.shape[dim] - width, cells.shape[dim], axis=dim)
        cells = jnp.concatenate(
            [
                lax.ppermute(tail, axis, [(i, (i + 1) % count) for i in range(ends)]),
                cells,
                lax.ppermute(head, axis, [((i + 1) % count, i) for i in range(ends)]),
            ],
            axis=dim,
        )
    return cells


def upwind(field, back_two, back_one, ahead_one, ahead_two, speed):
    behind = 1.5 * field - 2.0 * back_one + 0.5 * back_two
    ahead = -1.5 * field + 2.0 * ahead_one - 0.5 * ahead_two
    return jnp.maximum(speed, 0.0) * behind + jnp.minimum(speed, 0.0) * ahead


def reduced(first_vals, last_vals, tips):
    count = first_vals.shape[0]
    prev_q = jnp.zeros((), jnp.float32)
    prev_last = jnp.zeros_like(first_vals[0])
    fronts, backs, front_qs, back_qs = ([], [], [], [])
    for block in range(count):
        head_v = tips[0][block]
        tail_v = tips[1][block]
        head_w = tips[2][block]
        tail_w = tips[3][block]
        pivot = 1.0 - head_v * prev_q
        front = (first_vals[block] - head_v * prev_last) / pivot
        back = last_vals[block] - tail_v * prev_last + tail_v * prev_q * front
        front_q = head_w / pivot
        back_q = tail_w + tail_v * prev_q * front_q
        fronts.append(front)
        backs.append(back)
        front_qs.append(front_q)
        back_qs.append(back_q)
        prev_q = back_q
        prev_last = back
    heads = [None] * count
    tails = [None] * count
    heads[count - 1] = fronts[count - 1]
    tails[count - 1] = backs[count - 1]
    for block in range(count - 2, -1, -1):
        after = heads[block + 1]
        heads[block] = fronts[block] - front_qs[block] * after
        tails[block] = backs[block] - back_qs[block] * after
    zero = jnp.zeros_like(first_vals[0])
    lower_prev = jnp.stack([zero] + tails[:-1])
    upper_next = jnp.stack(heads[1:] + [zero])
    return (lower_prev, upper_next)


def body(velocity, stiffness, block_inverse):
    blocks = lax.axis_size("gy")
    own_index = lax.axis_index("gy")
    spans = velocity.shape[3]
    stiff = stiffness[0]
    first_flag = (own_index > 0).astype(jnp.float32)
    last_flag = (own_index < blocks - 1).astype(jnp.float32)
    coupling = -jnp.array(implicit_share, jnp.float32) * stiff
    lower = coupling * first_flag
    upper = coupling * last_flag
    column_v = block_inverse[:, :, 0] * lower[:, None]
    column_w = block_inverse[:, :, -1] * upper[:, None]
    own_tips = jnp.stack(
        [column_v[:, 0], column_v[:, -1], column_w[:, 0], column_w[:, -1]], axis=1
    )[:, :, None]
    every_tip = lax.all_gather(own_tips, "gy", axis=2, tiled=True)
    current = velocity
    previous = velocity
    for step in range(SUBSTEPS):
        widened = with_halo(current, (("gx", 1),), 2, True)
        middle = widened[:, 2:-2]
        ypadded = with_halo(middle, (("gy", 2),), 2, False)
        along_x = upwind(
            middle,
            widened[:, 0:-4],
            widened[:, 1:-3],
            widened[:, 3:-1],
            widened[:, 4:],
            middle[0:1],
        )
        along_y = upwind(
            middle,
            ypadded[:, :, 0:-4],
            ypadded[:, :, 1:-3],
            ypadded[:, :, 3:-1],
            ypadded[:, :, 4:],
            middle[1:2],
        )
        along_z = upwind(
            middle,
            jnp.roll(middle, 2, 3),
            jnp.roll(middle, 1, 3),
            jnp.roll(middle, -1, 3),
            jnp.roll(middle, -2, 3),
            middle[2:3],
        )
        advect = courant[0] * along_x + courant[1] * along_y + courant[2] * along_z
        diffuse = stiff * (ypadded[:, :, 3:-1] - 2.0 * middle + ypadded[:, :, 1:-3])
        forcing = middle + implicit_share[step] * diffuse - new_weight[step] * advect
        if step > 0:
            forcing = forcing - old_weight[step] * previous
        previous = advect
        planes = middle.shape[1]
        solved = jnp.einsum(
            "ij,cxjz->cxiz", block_inverse[step], forcing, precision=lax.Precision.HIGHEST
        )
        edges = jnp.stack([solved[:, :, 0, :], solved[:, :, -1, :]]).reshape(2, -1)
        tips = every_tip[step]
        grouped = lax.all_to_all(
            edges.reshape(2, blocks, -1), "gy", split_axis=1, concat_axis=1, tiled=True
        )
        lower_prev, upper_next = reduced(grouped[0], grouped[1], tips)
        returned = lax.all_to_all(
            jnp.stack([lower_prev, upper_next]), "gy", split_axis=1, concat_axis=1, tiled=True
        ).reshape(2, -1)
        lower_own = returned[0]
        upper_own = returned[1]
        lower_own = lower_own.reshape(3, planes, spans)[:, :, None, :]
        upper_own = upper_own.reshape(3, planes, spans)[:, :, None, :]
        current = (
            solved
            - column_v[step][None, None, :, None] * lower_own
            - column_w[step][None, None, :, None] * upper_own
        )
    return current


def solution(mesh):
    return jax.shard_map(
        body,
        mesh=mesh,
        in_specs=(P(None, "gx", "gy", None), P("gy"), P(None, "gy", None)),
        out_specs=P(None, "gx", "gy", None),
        check_vma=False,
    )
```

profile of v0, /device:TPU:8, one launch (start us, length us, event | category | flops | bytes accessed | tf_op | source)
XLA Modules:
  0.0 241.1 jit_solution(6409454955614664541)
XLA Ops:
  0.0 12.6 %collective-permute-start.3 = (f32[3,2,192,128]{3,2,1,0:T(8,128)}, f32[3,2,192,128]{3,2,1,0:T(8,128)}, u32[]{:S(2)}, u32[]{:S(2)}) collective-permute-start(f32[3,2,192,128]{3,2,1,0:T(8,128)} %param.4), channel_id=1, source_target_pairs={{8,0},{16,8},{24,16},{32,24},{40,32},{48,40},{56,48},{64,56},{72,6... | collective-permute-start | bytes 1769480 | tf_op jit(solution)/shard_map/ppermute | solution.py:23
  12.6 1.9 collective-permute-start.2
  14.5 0.8 fusion.335
  15.3 2.3 collective-permute-start
  17.6 3.6 %collective-permute-start.1 = (f32[3,2,2,128]{3,2,1,0:T(2,128)S(1)}, f32[3,2,2,128]{3,2,1,0:T(2,128)S(1)}, u32[]{:S(2)}, u32[]{:S(2)}) collective-permute-start(f32[3,2,2,128]{3,2,1,0:T(2,128)S(1)} %get-tuple-element.146), channel_id=1, source_target_pairs={{0,1},{1,2},{2,3},{3,4},{4,5},{5,6},{6,7},{8,9},{9,10},{10,11},{11... | collective-permute-start | bytes 18440 | tf_op jit(solution)/shard_map/ppermute | solution.py:21
  21.3 1.5 fusion.333
  23.0 1.2 fusion.331
  24.2 1.0 maximum_bitcast_fusion.8
  26.4 0.7 copy-done.20
  28.6 23.4 %all_gather.3 = f32[3,4,8]{1,0,2:T(4,128)S(1)} all-gather(f32[3,4,1]{1,0,2:T(4,128)S(1)} %maximum_bitcast_fusion.9), channel_id=1, replica_groups=mesh['gx'=64,'gy'=8] {'gy'}, dimensions={2}, use_global_device_ids=true | all-gather | bytes 432 | tf_op jit(solution)/shard_map/all_gather | solution.py:86
  52.3 0.7 fusion.339
  54.3 2.7 %fusion.61 = f32[3,2,192,128]{3,2,1,0:T(8,128)S(1)} fusion(f32[3,2,194,128]{3,2,1,0:T(8,128)S(1)} %constant_dynamic-update-slice_fusion, f32[3,2,192,128]{3,2,1,0:T(8,128)S(1)} %copy-done, f32[3,2,2,128]{3,2,1,0:T(2,128)S(1)} %copy-done.12, f32[3,2,192,128]{3,2,1,0:T(8,128)} %collective-permute-done.3, f32[3,2,192,128]{3,2,1,0:T(8,128)} %collective-permute-done.2, ...), kind=kLoop, calls=%fused_computation.79 | loop fusion | flops 7077888 | bytes 7084032 | tf_op jit(solution)/shard_map/add | solution.py:117
  57.1 1.8 convolution_bitcast_fusion.2
  59.7 5.2 %all-to-all-start = ((f32[2,8,96]{2,0,1:T(2,128)}), f32[2,8,96]{2,0,1:T(2,128)S(1)}, u32[]{:S(2)}, u32[]{:S(2)}) async-start(f32[2,8,96]{2,0,1:T(2,128)} %pad_maximum_fusion.11), calls=%async_computation | async-start | bytes 16384 | tf_op jit(solution)/shard_map/all_to_all | solution.py:129
  64.9 0.7 fusion.340
  83.8 7.7 %fusion.235 = (f32[1,96]{1,0:T(1,128)S(1)}, f32[1,96]{1,0:T(1,128)S(1)}, f32[1,96]{1,0:T(1,128)S(1)}, f32[1,96]{1,0:T(1,128)S(1)}, f32[1,96]{1,0:T(1,128)S(1)}, ...) fusion(f32[2,8,96]{2,0,1:T(2,128)S(1)} %all-to-all-done, ...), kind=kLoop, calls=%fused_computation.345 | loop fusion | flops 4512 | bytes 10476 | tf_op jit(solution)/shard_map/add | solution.py:48
  91.5 0.6 multiply_subtract_fusion.31
  92.9 7.2 %all-to-all-start.1 = ((f32[2,8,96]{2,0,1:T(2,128)}), f32[2,8,96]{2,0,1:T(2,128)S(1)}, u32[]{:S(2)}, u32[]{:S(2)}) async-start(f32[2,8,96]{2,0,1:T(2,128)} %copy.10), calls=%async_computation.1 | async-start | bytes 16384 | tf_op jit(solution)/shard_map/all_to_all | solution.py:133
  100.1 0.7 fusion.337
  100.8 5.6 %all-to-all-done.1 = f32[2,8,96]{2,0,1:T(2,128)S(1)} async-done(((f32[2,8,96]{2,0,1:T(2,128)}), f32[2,8,96]{2,0,1:T(2,128)S(1)}, u32[]{:S(2)}, u32[]{:S(2)}) %all-to-all-start.1) | async-done | bytes 6176 | tf_op jit(solution)/shard_map/all_to_all | solution.py:133
  106.6 0.7 copy-done.18
  107.4 1.9 collective-permute-start.7
  109.4 2.4 collective-permute-start.6
  112.5 3.3 %collective-permute-start.4 = (f32[3,2,2,128]{3,2,1,0:T(2,128)S(1)}, f32[3,2,2,128]{3,2,1,0:T(2,128)S(1)}, u32[]{:S(2)}, u32[]{:S(2)}) collective-permute-start(f32[3,2,2,128]{3,2,1,0:T(2,128)S(1)} %get-tuple-element.129), channel_id=1, source_target_pairs={{1,0},{2,1},{3,2},{4,3},{5,4},{6,5},{7,6},{9,8},{10,9},{11,10},{12... | collective-permute-start | bytes 18440 | tf_op jit(solution)/shard_map/ppermute | solution.py:23
  115.8 2.5 %collective-permute-start.5 = (f32[3,2,2,128]{3,2,1,0:T(2,128)S(1)}, f32[3,2,2,128]{3,2,1,0:T(2,128)S(1)}, u32[]{:S(2)}, u32[]{:S(2)}) collective-permute-start(f32[3,2,2,128]{3,2,1,0:T(2,128)S(1)} %get-tuple-element.128), channel_id=1, source_target_pairs={{0,1},{1,2},{2,3},{3,4},{4,5},{5,6},{6,7},{8,9},{9,10},{10,11},{11... | collective-permute-start | bytes 18440 | tf_op jit(solution)/shard_map/ppermute | solution.py:21
  118.6 2.7 %collective-permute-done.5 = f32[3,2,2,128]{3,2,1,0:T(2,128)S(1)} collective-permute-done((f32[3,2,2,128]{3,2,1,0:T(2,128)S(1)}, f32[3,2,2,128]{3,2,1,0:T(2,128)S(1)}, u32[]{:S(2)}, u32[]{:S(2)}) %collective-permute-start.5) | collective-permute-done | bytes 6176 | tf_op jit(solution)/shard_map/ppermute | solution.py:21
  121.3 2.5 %collective-permute-done.6 = f32[3,2,192,128]{3,2,1,0:T(8,128)S(1)} collective-permute-done((f32[3,2,192,128]{3,2,1,0:T(8,128)S(1)}, f32[3,2,192,128]{3,2,1,0:T(8,128)S(1)}, u32[]{:S(2)}, u32[]{:S(2)}) %collective-permute-start.6) | collective-permute-done | bytes 589856 | tf_op jit(solution)/shard_map/ppermute | solution.py:21
  123.9 1.3 fusion.42
  125.2 1.0 convolution_bitcast_fusion.1
  127.0 4.7 %all-to-all-start.2 = ((f32[2,8,96]{2,0,1:T(2,128)}), f32[2,8,96]{2,0,1:T(2,128)S(1)}, u32[]{:S(2)}, u32[]{:S(2)}) async-start(f32[2,8,96]{2,0,1:T(2,128)} %pad_maximum_fusion.13), calls=%async_computation.2 | async-start | bytes 16384 | tf_op jit(solution)/shard_map/all_to_all | solution.py:129
  131.7 0.7 fusion.338
  150.5 7.5 %fusion.206 = (f32[1,96]{1,0:T(1,128)S(1)}, f32[1,96]{1,0:T(1,128)S(1)}, f32[1,96]{1,0:T(1,128)S(1)}, f32[1,96]{1,0:T(1,128)S(1)}, f32[1,96]{1,0:T(1,128)S(1)}, ...) fusion(f32[2,8,96]{2,0,1:T(2,128)S(1)} %all-to-all-done.2, ...), kind=kLoop, calls=%fused_computation.301 | loop fusion | flops 4512 | bytes 10476 | tf_op jit(solution)/shard_map/add | solution.py:48
  158.8 13.3 %all_to_all.30 = f32[2,8,96]{2,0,1:T(2,128)S(1)} all-to-all(f32[2,8,96]{2,0,1:T(2,128)S(1)} %copy.13), channel_id=1, replica_groups=mesh['gx'=64,'gy'=8] {'gy'}, dimensions={1} | all-to-all | bytes 12288 | tf_op jit(solution)/shard_map/all_to_all | solution.py:133
  172.3 0.7 copy-done.16
  173.2 1.9 collective-permute-start.11
  175.1 2.4 collective-permute-start.10
  178.2 3.3 %collective-permute-start.8 = (f32[3,2,2,128]{3,2,1,0:T(2,128)S(1)}, f32[3,2,2,128]{3,2,1,0:T(2,128)S(1)}, u32[]{:S(2)}, u32[]{:S(2)}) collective-permute-start(f32[3,2,2,128]{3,2,1,0:T(2,128)S(1)} %get-tuple-element.113), channel_id=1, source_target_pairs={{1,0},{2,1},{3,2},{4,3},{5,4},{6,5},{7,6},{9,8},{10,9},{11,10},{12... | collective-permute-start | bytes 18440 | tf_op jit(solution)/shard_map/ppermute | solution.py:23
  181.5 2.7 %collective-permute-start.9 = (f32[3,2,2,128]{3,2,1,0:T(2,128)S(1)}, f32[3,2,2,128]{3,2,1,0:T(2,128)S(1)}, u32[]{:S(2)}, u32[]{:S(2)}) collective-permute-start(f32[3,2,2,128]{3,2,1,0:T(2,128)S(1)} %get-tuple-element.112), channel_id=1, source_target_pairs={{0,1},{1,2},{2,3},{3,4},{4,5},{5,6},{6,7},{8,9},{9,10},{10,11},{11... | collective-permute-start | bytes 18440 | tf_op jit(solution)/shard_map/ppermute | solution.py:21
  184.6 2.5 %collective-permute-done.9 = f32[3,2,2,128]{3,2,1,0:T(2,128)S(1)} collective-permute-done((f32[3,2,2,128]{3,2,1,0:T(2,128)S(1)}, f32[3,2,2,128]{3,2,1,0:T(2,128)S(1)}, u32[]{:S(2)}, u32[]{:S(2)}) %collective-permute-start.9) | collective-permute-done | bytes 6176 | tf_op jit(solution)/shard_map/ppermute | solution.py:21
  187.1 2.5 %collective-permute-done.10 = f32[3,2,192,128]{3,2,1,0:T(8,128)S(1)} collective-permute-done((f32[3,2,192,128]{3,2,1,0:T(8,128)S(1)}, f32[3,2,192,128]{3,2,1,0:T(8,128)S(1)}, u32[]{:S(2)}, u32[]{:S(2)}) %collective-permute-start.10) | collective-permute-done | bytes 589856 | tf_op jit(solution)/shard_map/ppermute | solution.py:21
  189.6 2.3 convolution_bitcast_fusion
  192.7 4.7 %all-to-all-start.4 = ((f32[2,8,96]{2,0,1:T(2,128)}), f32[2,8,96]{2,0,1:T(2,128)S(1)}, u32[]{:S(2)}, u32[]{:S(2)}) async-start(f32[2,8,96]{2,0,1:T(2,128)} %pad_maximum_fusion.15), calls=%async_computation.4 | async-start | bytes 16384 | tf_op jit(solution)/shard_map/all_to_all | solution.py:129
  197.4 0.7 fusion.336
  216.3 7.6 %fusion.177 = (f32[1,96]{1,0:T(1,128)S(1)}, f32[1,96]{1,0:T(1,128)S(1)}, f32[1,96]{1,0:T(1,128)S(1)}, f32[1,96]{1,0:T(1,128)S(1)}, f32[1,96]{1,0:T(1,128)S(1)}, ...) fusion(f32[2,8,96]{2,0,1:T(2,128)S(1)} %all-to-all-done.4, ...), kind=kLoop, calls=%fused_computation.257 | loop fusion | flops 4512 | bytes 10476 | tf_op jit(solution)/shard_map/add | solution.py:48
  224.6 0.7 copy-done.14
  225.3 13.3 %all_to_all.31 = f32[2,8,96]{2,0,1:T(2,128)S(1)} all-to-all(f32[2,8,96]{2,0,1:T(2,128)S(1)} %copy.16), channel_id=1, replica_groups=mesh['gx'=64,'gy'=8] {'gy'}, dimensions={1} | all-to-all | bytes 12288 | tf_op jit(solution)/shard_map/all_to_all | solution.py:133
  238.8 0.6 copy-done.15
  239.4 1.7 multiply_subtract_fusion.4
  (129 shorter events, 11.2 us)
Async XLA Ops:
  0.0 53.1 %collective-permute-start.3 = (f32[3,2,192,128]{3,2,1,0:T(8,128)}, f32[3,2,192,128]{3,2,1,0:T(8,128)}, u32[]{:S(2)}, u32[]{:S(2)}) collective-permute-start(f32[3,2,192,128]{3,2,1,0:T(8,128)} %param.4), channel_id=1, source_target_pairs={{8,0},{16,8},{24,16},{32,24},{40,32},{48,40},{56,48},{64,56},{72,6... | collective-permute-start | bytes 1769480 | tf_op jit(solution)/shard_map/ppermute | solution.py:23
  12.6 40.5 %collective-permute-start.2 = (f32[3,2,192,128]{3,2,1,0:T(8,128)}, f32[3,2,192,128]{3,2,1,0:T(8,128)}, u32[]{:S(2)}, u32[]{:S(2)}) collective-permute-start(f32[3,2,192,128]{3,2,1,0:T(8,128)} %param.4), channel_id=1, source_target_pairs={{0,8},{8,16},{16,24},{24,32},{32,40},{40,48},{48,56},{56,64},{64,7... | collective-permute-start | bytes 1769480 | tf_op jit(solution)/shard_map/ppermute | solution.py:21
  15.3 37.7 %collective-permute-start = (f32[3,2,2,128]{3,2,1,0:T(2,128)S(1)}, f32[3,2,2,128]{3,2,1,0:T(2,128)S(1)}, u32[]{:S(2)}, u32[]{:S(2)}) collective-permute-start(f32[3,2,2,128]{3,2,1,0:T(2,128)S(1)} %get-tuple-element.147), channel_id=1, source_target_pairs={{1,0},{2,1},{3,2},{4,3},{5,4},{6,5},{7,6},{9,8},{10,9},{11,10},{12... | collective-permute-start | bytes 18440 | tf_op jit(solution)/shard_map/ppermute | solution.py:23
  17.6 5.2 %copy-start = (f32[3,2,192,128]{3,2,1,0:T(8,128)S(1)}, f32[3,2,192,128]{3,2,1,0:T(8,128)}, u32[]{:S(2)}) copy-start(f32[3,2,192,128]{3,2,1,0:T(8,128)} %param.4) | copy-start | bytes 1769476
  17.6 35.4 %collective-permute-start.1 = (f32[3,2,2,128]{3,2,1,0:T(2,128)S(1)}, f32[3,2,2,128]{3,2,1,0:T(2,128)S(1)}, u32[]{:S(2)}, u32[]{:S(2)}) collective-permute-start(f32[3,2,2,128]{3,2,1,0:T(2,128)S(1)} %get-tuple-element.146), channel_id=1, source_target_pairs={{0,1},{1,2},{2,3},{3,4},{4,5},{5,6},{6,7},{8,9},{9,10},{10,11},{11... | collective-permute-start | bytes 18440 | tf_op jit(solution)/shard_map/ppermute | solution.py:21
  24.2 1.7 copy-start.3
  26.4 0.7 copy-start.20
  52.0 1.7 copy-start.1
  52.0 1.6 copy-start.2
  52.0 1.6 copy-start.5
  52.0 1.6 copy-start.6
  52.0 1.6 copy-start.7
  52.0 1.6 copy-start.8
  52.1 1.6 copy-start.9
  52.1 1.6 copy-start.10
  53.0 0.6 copy-start.11
  53.6 0.7 copy-start.12
  59.7 24.0 %all-to-all-start = ((f32[2,8,96]{2,0,1:T(2,128)}), f32[2,8,96]{2,0,1:T(2,128)S(1)}, u32[]{:S(2)}, u32[]{:S(2)}) async-start(f32[2,8,96]{2,0,1:T(2,128)} %pad_maximum_fusion.11), calls=%async_computation | async-start | bytes 16384 | tf_op jit(solution)/shard_map/all_to_all | solution.py:129
  92.2 14.4 %copy-start.19 = (f32[1,192]{1,0:T(1,128)S(1)}, f32[1,192]{1,0:T(1,128)}, u32[]{:S(2)}) copy-start(f32[1,192]{1,0:T(1,128)} %get-tuple-element.237) | copy-start | bytes 2308
  92.2 66.5 %copy-start.13 = (f32[1,96]{1,0:T(1,128)}, f32[1,96]{1,0:T(1,128)S(1)}, u32[]{:S(2)}) copy-start(f32[1,96]{1,0:T(1,128)S(1)} %broadcast.6105) | copy-start | bytes 1156
  92.9 13.5 %all-to-all-start.1 = ((f32[2,8,96]{2,0,1:T(2,128)}), f32[2,8,96]{2,0,1:T(2,128)S(1)}, u32[]{:S(2)}, u32[]{:S(2)}) async-start(f32[2,8,96]{2,0,1:T(2,128)} %copy.10), calls=%async_computation.1 | async-start | bytes 16384 | tf_op jit(solution)/shard_map/all_to_all | solution.py:133
  106.6 0.7 copy-start.18
  107.4 13.9 %collective-permute-start.7 = (f32[3,2,192,128]{3,2,1,0:T(8,128)S(1)}, f32[3,2,192,128]{3,2,1,0:T(8,128)S(1)}, u32[]{:S(2)}, u32[]{:S(2)}) collective-permute-start(f32[3,2,192,128]{3,2,1,0:T(8,128)S(1)} %multiply_subtract_fusion.6), channel_id=1, source_target_pairs={{8,0},{16,8},{24,16},{32,24},{40,32},{48,40},{56,48},{64,56},{72,6... | collective-permute-start | bytes 1769480 | tf_op jit(solution)/shard_map/ppermute | solution.py:23
  109.4 14.5 %collective-permute-start.6 = (f32[3,2,192,128]{3,2,1,0:T(8,128)S(1)}, f32[3,2,192,128]{3,2,1,0:T(8,128)S(1)}, u32[]{:S(2)}, u32[]{:S(2)}) collective-permute-start(f32[3,2,192,128]{3,2,1,0:T(8,128)S(1)} %multiply_subtract_fusion.6), channel_id=1, source_target_pairs={{0,8},{8,16},{16,24},{24,32},{32,40},{40,48},{48,56},{56,64},{64,7... | collective-permute-start | bytes 1769480 | tf_op jit(solution)/shard_map/ppermute | solution.py:21
  112.5 6.2 %collective-permute-start.4 = (f32[3,2,2,128]{3,2,1,0:T(2,128)S(1)}, f32[3,2,2,128]{3,2,1,0:T(2,128)S(1)}, u32[]{:S(2)}, u32[]{:S(2)}) collective-permute-start(f32[3,2,2,128]{3,2,1,0:T(2,128)S(1)} %get-tuple-element.129), channel_id=1, source_target_pairs={{1,0},{2,1},{3,2},{4,3},{5,4},{6,5},{7,6},{9,8},{10,9},{11,10},{12... | collective-permute-start | bytes 18440 | tf_op jit(solution)/shard_map/ppermute | solution.py:23
  115.8 5.5 %collective-permute-start.5 = (f32[3,2,2,128]{3,2,1,0:T(2,128)S(1)}, f32[3,2,2,128]{3,2,1,0:T(2,128)S(1)}, u32[]{:S(2)}, u32[]{:S(2)}) collective-permute-start(f32[3,2,2,128]{3,2,1,0:T(2,128)S(1)} %get-tuple-element.128), channel_id=1, source_target_pairs={{0,1},{1,2},{2,3},{3,4},{4,5},{5,6},{6,7},{8,9},{9,10},{10,11},{11... | collective-permute-start | bytes 18440 | tf_op jit(solution)/shard_map/ppermute | solution.py:21
  123.9 1.3 copy-start.4
  127.0 23.5 %all-to-all-start.2 = ((f32[2,8,96]{2,0,1:T(2,128)}), f32[2,8,96]{2,0,1:T(2,128)S(1)}, u32[]{:S(2)}, u32[]{:S(2)}) async-start(f32[2,8,96]{2,0,1:T(2,128)} %pad_maximum_fusion.13), calls=%async_computation.2 | async-start | bytes 16384 | tf_op jit(solution)/shard_map/all_to_all | solution.py:129
  133.7 38.6 %copy-start.17 = (f32[1,192]{1,0:T(1,128)S(1)}, f32[1,192]{1,0:T(1,128)}, u32[]{:S(2)}) copy-start(f32[1,192]{1,0:T(1,128)} %get-tuple-element.236) | copy-start | bytes 2308
  172.3 0.7 copy-start.16
  173.2 13.9 %collective-permute-start.11 = (f32[3,2,192,128]{3,2,1,0:T(8,128)S(1)}, f32[3,2,192,128]{3,2,1,0:T(8,128)S(1)}, u32[]{:S(2)}, u32[]{:S(2)}) collective-permute-start(f32[3,2,192,128]{3,2,1,0:T(8,128)S(1)} %multiply_subtract_fusion.5), channel_id=1, source_target_pairs={{8,0},{16,8},{24,16},{32,24},{40,32},{48,40},{56,48},{64,56},{72,6... | collective-permute-start | bytes 1769480 | tf_op jit(solution)/shard_map/ppermute | solution.py:23
  175.1 14.5 %collective-permute-start.10 = (f32[3,2,192,128]{3,2,1,0:T(8,128)S(1)}, f32[3,2,192,128]{3,2,1,0:T(8,128)S(1)}, u32[]{:S(2)}, u32[]{:S(2)}) collective-permute-start(f32[3,2,192,128]{3,2,1,0:T(8,128)S(1)} %multiply_subtract_fusion.5), channel_id=1, source_target_pairs={{0,8},{8,16},{16,24},{24,32},{32,40},{40,48},{48,56},{56,64},{64,7... | collective-permute-start | bytes 1769480 | tf_op jit(solution)/shard_map/ppermute | solution.py:21
  178.2 6.4 %collective-permute-start.8 = (f32[3,2,2,128]{3,2,1,0:T(2,128)S(1)}, f32[3,2,2,128]{3,2,1,0:T(2,128)S(1)}, u32[]{:S(2)}, u32[]{:S(2)}) collective-permute-start(f32[3,2,2,128]{3,2,1,0:T(2,128)S(1)} %get-tuple-element.113), channel_id=1, source_target_pairs={{1,0},{2,1},{3,2},{4,3},{5,4},{6,5},{7,6},{9,8},{10,9},{11,10},{12... | collective-permute-start | bytes 18440 | tf_op jit(solution)/shard_map/ppermute | solution.py:23
  181.5 5.5 %collective-permute-start.9 = (f32[3,2,2,128]{3,2,1,0:T(2,128)S(1)}, f32[3,2,2,128]{3,2,1,0:T(2,128)S(1)}, u32[]{:S(2)}, u32[]{:S(2)}) collective-permute-start(f32[3,2,2,128]{3,2,1,0:T(2,128)S(1)} %get-tuple-element.112), channel_id=1, source_target_pairs={{0,1},{1,2},{2,3},{3,4},{4,5},{5,6},{6,7},{8,9},{9,10},{10,11},{11... | collective-permute-start | bytes 18440 | tf_op jit(solution)/shard_map/ppermute | solution.py:21
  192.7 23.6 %all-to-all-start.4 = ((f32[2,8,96]{2,0,1:T(2,128)}), f32[2,8,96]{2,0,1:T(2,128)S(1)}, u32[]{:S(2)}, u32[]{:S(2)}) async-start(f32[2,8,96]{2,0,1:T(2,128)} %pad_maximum_fusion.15), calls=%async_computation.4 | async-start | bytes 16384 | tf_op jit(solution)/shard_map/all_to_all | solution.py:129
  224.6 0.7 copy-start.14
  238.8 0.6 copy-start.15
where the time goes:
time: 243 us; the launch traced here: 241 us
  starting transfers between devices  62.7 us (26%)
  between operations  55.7 us (23%)
  blocking collectives  50 us (21%)
  other arithmetic  34.1 us (14%)
  local copies, waits for them, and re-layouts  17.6 us (7%)
  waiting for transfers between devices  15.9 us (7%)
  matrix products  5.06 us (2%)
    all_to_all x2, blocking collectives, body(): lax.all_to_all(jnp.stack([lower_prev, upper_next]), 'gy', split_axis=1, c...  26.6 us
    ppermute x6, starting transfers between devices, with_halo(): lax.ppermute(head, axis, [((i + 1) % count, i) for i in range(ends)])  25.5 us
    all_gather x1, blocking collectives, body(): every_tip = lax.all_gather(own_tips, 'gy', axis=2, tiled=True)  23.4 us
    add x3, other arithmetic, reduced(): back = last_vals[block] - tail_v * prev_last + tail_v * prev_q * front  22.8 us
    ppermute x6, starting transfers between devices, with_halo(): lax.ppermute(tail, axis, [(i, (i + 1) % count) for i in range(ends)])  15.5 us
    all_to_all x3, starting transfers between devices, body(): lax.all_to_all(edges.reshape(2, blocks, -1), 'gy', split_axis=1, concat_a...  14.6 us
    ppermute x6, waiting for transfers between devices, with_halo(): lax.ppermute(tail, axis, [(i, (i + 1) % count) for i in range(ends)])  10.3 us
    all_to_all x1, starting transfers between devices, body(): lax.all_to_all(jnp.stack([lower_prev, upper_next]), 'gy', split_axis=1, c...  7.21 us
  transfers between devices with their start and end apart: 16, of which 5 were waited for; matrix products, arithmetic and copies ran while one was open for 5% of the time, Pallas kernels for 0%

commit v1 on v0

--- a/solution.py
+++ b/solution.py
@@ -83,7 +83,9 @@
     own_tips = jnp.stack(
         [column_v[:, 0], column_v[:, -1], column_w[:, 0], column_w[:, -1]], axis=1
     )[:, :, None]
-    every_tip = lax.all_gather(own_tips, "gy", axis=2, tiled=True)
+    every_tip = jnp.concatenate(
+        lax.all_to_all(jnp.stack([own_tips] * lax.axis_size("gy")), "gy", 0, 0), axis=2
+    )
     current = velocity
     previous = velocity
     for step in range(SUBSTEPS):

time: 243 us -> 228 us (0.938)
  blocking collectives: 50 us -> 26.6 us
  starting transfers between devices: 62.7 us -> 72.1 us
  local copies, waits for them, and re-layouts: 17.6 us -> 14.9 us
    all_gather x1 -> x0, blocking collectives: 23.4 us -> none  [body(): every_tip = lax.all_gather(own_tips, 'gy', axis=2, tiled=True)]
    all_to_all x0 -> x1, starting transfers between devices: none -> 7.55 us  [body(): lax.all_to_all(jnp.stack([own_tips] * lax.axis_size('gy')), 'gy', 0, 0)]
    unnamed x44 -> x8, local copies, waits for them, and re-layouts: 4.78 us -> 0.9 us
  transfers between devices with their start and end apart: 16 -> 17, of which waited for: 5 -> 6; matrix products, arithmetic and copies ran while one was open for 5% -> 6% of each run, Pallas kernels for 0% -> 0%
where the time goes in v1:
time: 228 us; the launch traced here: 226 us
  starting transfers between devices  72.1 us (32%)
  between operations  55.3 us (24%)
  other arithmetic  34.2 us (15%)
  blocking collectives  26.6 us (12%)
  waiting for transfers between devices  17.9 us (8%)
  local copies, waits for them, and re-layouts  14.9 us (7%)
  matrix products  5.06 us (2%)
    ppermute x6, starting transfers between devices, with_halo(): lax.ppermute(head, axis, [((i + 1) % count, i) for i in range(ends)])  27.4 us
    all_to_all x2, blocking collectives, body(): lax.all_to_all(jnp.stack([lower_prev, upper_next]), 'gy', split_axis=1, c...  26.6 us
    add x3, other arithmetic, reduced(): back = last_vals[block] - tail_v * prev_last + tail_v * prev_q * front  22.2 us
    all_to_all x3, starting transfers between devices, body(): lax.all_to_all(edges.reshape(2, blocks, -1), 'gy', split_axis=1, concat_a...  15 us
    ppermute x6, starting transfers between devices, with_halo(): lax.ppermute(tail, axis, [(i, (i + 1) % count) for i in range(ends)])  14.9 us
    ppermute x6, waiting for transfers between devices, with_halo(): lax.ppermute(tail, axis, [(i, (i + 1) % count) for i in range(ends)])  10.8 us
    all_to_all x1, starting transfers between devices, body(): lax.all_to_all(jnp.stack([own_tips] * lax.axis_size('gy')), 'gy', 0, 0)  7.55 us
    all_to_all x1, starting transfers between devices, body(): lax.all_to_all(jnp.stack([lower_prev, upper_next]), 'gy', split_axis=1, c...  7.21 us
  transfers between devices with their start and end apart: 17, of which 6 were waited for; matrix products, arithmetic and copies ran while one was open for 6% of the time, Pallas kernels for 0%

profile of v1, /device:TPU:8, one launch (start us, length us, event | category | flops | bytes accessed | tf_op | source)
XLA Modules:
  0.0 226.0 jit_solution(848122234377416777)
XLA Ops:
  0.0 12.6 %collective-permute-start.3 = (f32[3,2,192,128]{3,2,1,0:T(8,128)}, f32[3,2,192,128]{3,2,1,0:T(8,128)}, u32[]{:S(2)}, u32[]{:S(2)}) collective-permute-start(f32[3,2,192,128]{3,2,1,0:T(8,128)} %param.4), channel_id=1, source_target_pairs={{8,0},{16,8},{24,16},{32,24},{40,32},{48,40},{56,48},{64,56},{72,6... | collective-permute-start | bytes 1769480 | tf_op jit(solution)/shard_map/ppermute | solution.py:23
  12.6 1.9 collective-permute-start.2
  14.5 0.8 fusion.335
  15.3 2.3 %collective-permute-start = (f32[3,2,2,128]{3,2,1,0:T(2,128)S(1)}, f32[3,2,2,128]{3,2,1,0:T(2,128)S(1)}, u32[]{:S(2)}, u32[]{:S(2)}) collective-permute-start(f32[3,2,2,128]{3,2,1,0:T(2,128)S(1)} %get-tuple-element.147), channel_id=1, source_target_pairs={{1,0},{2,1},{3,2},{4,3},{5,4},{6,5},{7,6},{9,8},{10,9},{11,10},{12... | collective-permute-start | bytes 18440 | tf_op jit(solution)/shard_map/ppermute | solution.py:23
  17.6 3.5 %collective-permute-start.1 = (f32[3,2,2,128]{3,2,1,0:T(2,128)S(1)}, f32[3,2,2,128]{3,2,1,0:T(2,128)S(1)}, u32[]{:S(2)}, u32[]{:S(2)}) collective-permute-start(f32[3,2,2,128]{3,2,1,0:T(2,128)S(1)} %get-tuple-element.146), channel_id=1, source_target_pairs={{0,1},{1,2},{2,3},{3,4},{4,5},{5,6},{6,7},{8,9},{9,10},{10,11},{11... | collective-permute-start | bytes 18440 | tf_op jit(solution)/shard_map/ppermute | solution.py:21
  21.8 1.4 fusion.330
  25.0 7.5 %all-to-all-start.1 = ((f32[8,3,4,1]{2,3,1,0:T(1,128)}), f32[8,3,4,1]{2,3,1,0:T(1,128)S(1)}, u32[]{:S(2)}, u32[]{:S(2)}) async-start(f32[8,3,4,1]{2,3,1,0:T(1,128)} %stack.56), calls=%async_computation.1 | async-start | bytes 24576 | tf_op jit(solution)/shard_map/all_to_all | solution.py:87
  32.7 1.2 fusion.334
  33.9 1.2 fusion.331
  35.1 1.2 fusion.332
  36.3 0.9 maximum_bitcast_fusion.8
  37.3 1.5 all-to-all-done.1
  38.9 0.7 fusion.339
  39.6 4.0 %fusion.61 = f32[3,2,192,128]{3,2,1,0:T(8,128)S(1)} fusion(f32[3,2,194,128]{3,2,1,0:T(8,128)S(1)} %constant_dynamic-update-slice_fusion, f32[3,2,192,128]{3,2,1,0:T(8,128)S(1)} %copy-done, f32[3,2,2,128]{3,2,1,0:T(2,128)S(1)} %collective-permute-done.1, f32[3,2,192,128]{3,2,1,0:T(8,128)} %collective-permute-done.3, ...), kind=kLoop, calls=%fused_computation.79 | loop fusion | flops 7077888 | bytes 7084032 | tf_op jit(solution)/shard_map/add | solution.py:119
  43.6 1.8 convolution_bitcast_fusion.2
  46.3 5.7 %all-to-all-start = ((f32[2,8,96]{2,0,1:T(2,128)}), f32[2,8,96]{2,0,1:T(2,128)S(1)}, u32[]{:S(2)}, u32[]{:S(2)}) async-start(f32[2,8,96]{2,0,1:T(2,128)} %pad_maximum_fusion.11), calls=%async_computation | async-start | bytes 16384 | tf_op jit(solution)/shard_map/all_to_all | solution.py:131
  51.9 0.7 fusion.340
  70.6 7.3 %fusion.235 = (f32[1,96]{1,0:T(1,128)S(1)}, f32[1,96]{1,0:T(1,128)S(1)}, f32[1,96]{1,0:T(1,128)S(1)}, f32[1,96]{1,0:T(1,128)S(1)}, f32[1,96]{1,0:T(1,128)S(1)}, ...) fusion(f32[2,8,96]{2,0,1:T(2,128)S(1)} %all-to-all-done, ...), kind=kLoop, calls=%fused_computation.345 | loop fusion | flops 4512 | bytes 10476 | tf_op jit(solution)/shard_map/add | solution.py:48
  77.9 0.7 multiply_subtract_fusion.31
  79.4 7.2 %all-to-all-start.2 = ((f32[2,8,96]{2,0,1:T(2,128)}), f32[2,8,96]{2,0,1:T(2,128)S(1)}, u32[]{:S(2)}, u32[]{:S(2)}) async-start(f32[2,8,96]{2,0,1:T(2,128)} %copy.10), calls=%async_computation.2 | async-start | bytes 16384 | tf_op jit(solution)/shard_map/all_to_all | solution.py:135
  86.6 0.7 fusion.337
  87.3 5.6 %all-to-all-done.2 = f32[2,8,96]{2,0,1:T(2,128)S(1)} async-done(((f32[2,8,96]{2,0,1:T(2,128)}), f32[2,8,96]{2,0,1:T(2,128)S(1)}, u32[]{:S(2)}, u32[]{:S(2)}) %all-to-all-start.2) | async-done | bytes 6176 | tf_op jit(solution)/shard_map/all_to_all | solution.py:135
  93.2 3.9 %collective-permute-start.7 = (f32[3,2,192,128]{3,2,1,0:T(8,128)S(1)}, f32[3,2,192,128]{3,2,1,0:T(8,128)S(1)}, u32[]{:S(2)}, u32[]{:S(2)}) collective-permute-start(f32[3,2,192,128]{3,2,1,0:T(8,128)S(1)} %multiply_subtract_fusion.6), channel_id=1, source_target_pairs={{8,0},{16,8},{24,16},{32,24},{40,32},{48,40},{56,48},{64,56},{72,6... | collective-permute-start | bytes 1769480 | tf_op jit(solution)/shard_map/ppermute | solution.py:23
  97.1 1.9 collective-permute-start.6
  99.7 3.3 %collective-permute-start.4 = (f32[3,2,2,128]{3,2,1,0:T(2,128)S(1)}, f32[3,2,2,128]{3,2,1,0:T(2,128)S(1)}, u32[]{:S(2)}, u32[]{:S(2)}) collective-permute-start(f32[3,2,2,128]{3,2,1,0:T(2,128)S(1)} %get-tuple-element.129), channel_id=1, source_target_pairs={{1,0},{2,1},{3,2},{4,3},{5,4},{6,5},{7,6},{9,8},{10,9},{11,10},{12... | collective-permute-start | bytes 18440 | tf_op jit(solution)/shard_map/ppermute | solution.py:23
  103.1 2.5 %collective-permute-start.5 = (f32[3,2,2,128]{3,2,1,0:T(2,128)S(1)}, f32[3,2,2,128]{3,2,1,0:T(2,128)S(1)}, u32[]{:S(2)}, u32[]{:S(2)}) collective-permute-start(f32[3,2,2,128]{3,2,1,0:T(2,128)S(1)} %get-tuple-element.128), channel_id=1, source_target_pairs={{0,1},{1,2},{2,3},{3,4},{4,5},{5,6},{6,7},{8,9},{9,10},{10,11},{11... | collective-permute-start | bytes 18440 | tf_op jit(solution)/shard_map/ppermute | solution.py:21
  105.9 2.7 %collective-permute-done.5 = f32[3,2,2,128]{3,2,1,0:T(2,128)S(1)} collective-permute-done((f32[3,2,2,128]{3,2,1,0:T(2,128)S(1)}, f32[3,2,2,128]{3,2,1,0:T(2,128)S(1)}, u32[]{:S(2)}, u32[]{:S(2)}) %collective-permute-start.5) | collective-permute-done | bytes 6176 | tf_op jit(solution)/shard_map/ppermute | solution.py:21
  108.6 3.0 %collective-permute-done.6 = f32[3,2,192,128]{3,2,1,0:T(8,128)S(1)} collective-permute-done((f32[3,2,192,128]{3,2,1,0:T(8,128)S(1)}, f32[3,2,192,128]{3,2,1,0:T(8,128)S(1)}, u32[]{:S(2)}, u32[]{:S(2)}) %collective-permute-start.6) | collective-permute-done | bytes 589856 | tf_op jit(solution)/shard_map/ppermute | solution.py:21
  111.6 1.3 fusion.42
  113.0 1.0 convolution_bitcast_fusion.1
  114.8 4.7 %all-to-all-start.3 = ((f32[2,8,96]{2,0,1:T(2,128)}), f32[2,8,96]{2,0,1:T(2,128)S(1)}, u32[]{:S(2)}, u32[]{:S(2)}) async-start(f32[2,8,96]{2,0,1:T(2,128)} %pad_maximum_fusion.13), calls=%async_computation.3 | async-start | bytes 16384 | tf_op jit(solution)/shard_map/all_to_all | solution.py:131
  119.4 0.7 fusion.338
  138.3 7.5 %fusion.206 = (f32[1,96]{1,0:T(1,128)S(1)}, f32[1,96]{1,0:T(1,128)S(1)}, f32[1,96]{1,0:T(1,128)S(1)}, f32[1,96]{1,0:T(1,128)S(1)}, f32[1,96]{1,0:T(1,128)S(1)}, ...) fusion(f32[2,8,96]{2,0,1:T(2,128)S(1)} %all-to-all-done.3, ...), kind=kLoop, calls=%fused_computation.301 | loop fusion | flops 4512 | bytes 10476 | tf_op jit(solution)/shard_map/add | solution.py:48
  145.8 0.7 multiply_subtract_fusion.19
  146.7 13.3 %all_to_all.35 = f32[2,8,96]{2,0,1:T(2,128)S(1)} all-to-all(f32[2,8,96]{2,0,1:T(2,128)S(1)} %copy.13), channel_id=1, replica_groups=mesh['gx'=64,'gy'=8] {'gy'}, dimensions={1} | all-to-all | bytes 12288 | tf_op jit(solution)/shard_map/all_to_all | solution.py:135
  160.4 1.9 collective-permute-start.11
  162.3 2.4 %collective-permute-start.10 = (f32[3,2,192,128]{3,2,1,0:T(8,128)S(1)}, f32[3,2,192,128]{3,2,1,0:T(8,128)S(1)}, u32[]{:S(2)}, u32[]{:S(2)}) collective-permute-start(f32[3,2,192,128]{3,2,1,0:T(8,128)S(1)} %multiply_subtract_fusion.5), channel_id=1, source_target_pairs={{0,8},{8,16},{16,24},{24,32},{32,40},{40,48},{48,56},{56,64},{64,7... | collective-permute-start | bytes 1769480 | tf_op jit(solution)/shard_map/ppermute | solution.py:21
  165.4 3.3 %collective-permute-start.8 = (f32[3,2,2,128]{3,2,1,0:T(2,128)S(1)}, f32[3,2,2,128]{3,2,1,0:T(2,128)S(1)}, u32[]{:S(2)}, u32[]{:S(2)}) collective-permute-start(f32[3,2,2,128]{3,2,1,0:T(2,128)S(1)} %get-tuple-element.113), channel_id=1, source_target_pairs={{1,0},{2,1},{3,2},{4,3},{5,4},{6,5},{7,6},{9,8},{10,9},{11,10},{12... | collective-permute-start | bytes 18440 | tf_op jit(solution)/shard_map/ppermute | solution.py:23
  168.8 2.7 %collective-permute-start.9 = (f32[3,2,2,128]{3,2,1,0:T(2,128)S(1)}, f32[3,2,2,128]{3,2,1,0:T(2,128)S(1)}, u32[]{:S(2)}, u32[]{:S(2)}) collective-permute-start(f32[3,2,2,128]{3,2,1,0:T(2,128)S(1)} %get-tuple-element.112), channel_id=1, source_target_pairs={{0,1},{1,2},{2,3},{3,4},{4,5},{5,6},{6,7},{8,9},{9,10},{10,11},{11... | collective-permute-start | bytes 18440 | tf_op jit(solution)/shard_map/ppermute | solution.py:21
  171.8 2.5 %collective-permute-done.9 = f32[3,2,2,128]{3,2,1,0:T(2,128)S(1)} collective-permute-done((f32[3,2,2,128]{3,2,1,0:T(2,128)S(1)}, f32[3,2,2,128]{3,2,1,0:T(2,128)S(1)}, u32[]{:S(2)}, u32[]{:S(2)}) %collective-permute-start.9) | collective-permute-done | bytes 6176 | tf_op jit(solution)/shard_map/ppermute | solution.py:21
  174.3 2.5 %collective-permute-done.10 = f32[3,2,192,128]{3,2,1,0:T(8,128)S(1)} collective-permute-done((f32[3,2,192,128]{3,2,1,0:T(8,128)S(1)}, f32[3,2,192,128]{3,2,1,0:T(8,128)S(1)}, u32[]{:S(2)}, u32[]{:S(2)}) %collective-permute-start.10) | collective-permute-done | bytes 589856 | tf_op jit(solution)/shard_map/ppermute | solution.py:21
  176.8 2.3 %convolution_bitcast_fusion = f32[3,2,192,128]{3,2,1,0:T(8,128)S(1)} fusion(f32[3,2,2,128]{3,2,1,0:T(2,128)S(1)} %collective-permute-done.8, f32[3,2,192,128]{3,2,1,0:T(8,128)S(1)} %multiply_subtract_fusion.5, f32[3,2,2,128]{3,2,1,0:T(2,128)S(1)} %collective-permute-done.9, f32[3,2,192,128]{3,2,1,0:T(8,128)S(1)} %collective-permute-done.11, ...), kind=kOutput, calls=%fused_computation | convolution fusion | flops 348585984 | bytes 9056260 | tf_op jit(solution)/shard_map/ij,cxjz->cxiz/dot_general | solution.py:126
  179.9 4.7 %all-to-all-start.5 = ((f32[2,8,96]{2,0,1:T(2,128)}), f32[2,8,96]{2,0,1:T(2,128)S(1)}, u32[]{:S(2)}, u32[]{:S(2)}) async-start(f32[2,8,96]{2,0,1:T(2,128)} %pad_maximum_fusion.15), calls=%async_computation.5 | async-start | bytes 16384 | tf_op jit(solution)/shard_map/all_to_all | solution.py:131
  184.6 0.7 fusion.336
  203.3 7.4 %fusion.177 = (f32[1,96]{1,0:T(1,128)S(1)}, f32[1,96]{1,0:T(1,128)S(1)}, f32[1,96]{1,0:T(1,128)S(1)}, f32[1,96]{1,0:T(1,128)S(1)}, f32[1,96]{1,0:T(1,128)S(1)}, ...) fusion(f32[2,8,96]{2,0,1:T(2,128)S(1)} %all-to-all-done.5, ...), kind=kLoop, calls=%fused_computation.257 | loop fusion | flops 4512 | bytes 10476 | tf_op jit(solution)/shard_map/add | solution.py:48
  210.7 0.7 multiply_subtract_fusion.7
  211.5 13.3 %all_to_all.36 = f32[2,8,96]{2,0,1:T(2,128)S(1)} all-to-all(f32[2,8,96]{2,0,1:T(2,128)S(1)} %copy.16), channel_id=1, replica_groups=mesh['gx'=64,'gy'=8] {'gy'}, dimensions={1} | all-to-all | bytes 12288 | tf_op jit(solution)/shard_map/all_to_all | solution.py:135
  225.0 1.0 multiply_subtract_fusion.4
  (95 shorter events, 8.4 us)
Async XLA Ops:
  0.0 39.6 %collective-permute-start.3 = (f32[3,2,192,128]{3,2,1,0:T(8,128)}, f32[3,2,192,128]{3,2,1,0:T(8,128)}, u32[]{:S(2)}, u32[]{:S(2)}) collective-permute-start(f32[3,2,192,128]{3,2,1,0:T(8,128)} %param.4), channel_id=1, source_target_pairs={{8,0},{16,8},{24,16},{32,24},{40,32},{48,40},{56,48},{64,56},{72,6... | collective-permute-start | bytes 1769480 | tf_op jit(solution)/shard_map/ppermute | solution.py:23
  12.6 27.0 %collective-permute-start.2 = (f32[3,2,192,128]{3,2,1,0:T(8,128)}, f32[3,2,192,128]{3,2,1,0:T(8,128)}, u32[]{:S(2)}, u32[]{:S(2)}) collective-permute-start(f32[3,2,192,128]{3,2,1,0:T(8,128)} %param.4), channel_id=1, source_target_pairs={{0,8},{8,16},{16,24},{24,32},{32,40},{40,48},{48,56},{56,64},{64,7... | collective-permute-start | bytes 1769480 | tf_op jit(solution)/shard_map/ppermute | solution.py:21
  15.3 24.3 %collective-permute-start = (f32[3,2,2,128]{3,2,1,0:T(2,128)S(1)}, f32[3,2,2,128]{3,2,1,0:T(2,128)S(1)}, u32[]{:S(2)}, u32[]{:S(2)}) collective-permute-start(f32[3,2,2,128]{3,2,1,0:T(2,128)S(1)} %get-tuple-element.147), channel_id=1, source_target_pairs={{1,0},{2,1},{3,2},{4,3},{5,4},{6,5},{7,6},{9,8},{10,9},{11,10},{12... | collective-permute-start | bytes 18440 | tf_op jit(solution)/shard_map/ppermute | solution.py:23
  17.6 22.0 %collective-permute-start.1 = (f32[3,2,2,128]{3,2,1,0:T(2,128)S(1)}, f32[3,2,2,128]{3,2,1,0:T(2,128)S(1)}, u32[]{:S(2)}, u32[]{:S(2)}) collective-permute-start(f32[3,2,2,128]{3,2,1,0:T(2,128)S(1)} %get-tuple-element.146), channel_id=1, source_target_pairs={{0,1},{1,2},{2,3},{3,4},{4,5},{5,6},{6,7},{8,9},{9,10},{10,11},{11... | collective-permute-start | bytes 18440 | tf_op jit(solution)/shard_map/ppermute | solution.py:21
  21.8 10.7 %copy-start = (f32[3,2,192,128]{3,2,1,0:T(8,128)S(1)}, f32[3,2,192,128]{3,2,1,0:T(8,128)}, u32[]{:S(2)}) copy-start(f32[3,2,192,128]{3,2,1,0:T(8,128)} %param.4) | copy-start | bytes 1769476
  23.4 0.7 copy-start.2
  25.0 13.9 %all-to-all-start.1 = ((f32[8,3,4,1]{2,3,1,0:T(1,128)}), f32[8,3,4,1]{2,3,1,0:T(1,128)S(1)}, u32[]{:S(2)}, u32[]{:S(2)}) async-start(f32[8,3,4,1]{2,3,1,0:T(1,128)} %stack.56), calls=%async_computation.1 | async-start | bytes 24576 | tf_op jit(solution)/shard_map/all_to_all | solution.py:87
  46.3 24.4 %all-to-all-start = ((f32[2,8,96]{2,0,1:T(2,128)}), f32[2,8,96]{2,0,1:T(2,128)S(1)}, u32[]{:S(2)}, u32[]{:S(2)}) async-start(f32[2,8,96]{2,0,1:T(2,128)} %pad_maximum_fusion.11), calls=%async_computation | async-start | bytes 16384 | tf_op jit(solution)/shard_map/all_to_all | solution.py:131
  79.4 13.5 %all-to-all-start.2 = ((f32[2,8,96]{2,0,1:T(2,128)}), f32[2,8,96]{2,0,1:T(2,128)S(1)}, u32[]{:S(2)}, u32[]{:S(2)}) async-start(f32[2,8,96]{2,0,1:T(2,128)} %copy.10), calls=%async_computation.2 | async-start | bytes 16384 | tf_op jit(solution)/shard_map/all_to_all | solution.py:135
  93.2 15.4 %collective-permute-start.7 = (f32[3,2,192,128]{3,2,1,0:T(8,128)S(1)}, f32[3,2,192,128]{3,2,1,0:T(8,128)S(1)}, u32[]{:S(2)}, u32[]{:S(2)}) collective-permute-start(f32[3,2,192,128]{3,2,1,0:T(8,128)S(1)} %multiply_subtract_fusion.6), channel_id=1, source_target_pairs={{8,0},{16,8},{24,16},{32,24},{40,32},{48,40},{56,48},{64,56},{72,6... | collective-permute-start | bytes 1769480 | tf_op jit(solution)/shard_map/ppermute | solution.py:23
  97.1 14.5 %collective-permute-start.6 = (f32[3,2,192,128]{3,2,1,0:T(8,128)S(1)}, f32[3,2,192,128]{3,2,1,0:T(8,128)S(1)}, u32[]{:S(2)}, u32[]{:S(2)}) collective-permute-start(f32[3,2,192,128]{3,2,1,0:T(8,128)S(1)} %multiply_subtract_fusion.6), channel_id=1, source_target_pairs={{0,8},{8,16},{16,24},{24,32},{32,40},{40,48},{48,56},{56,64},{64,7... | collective-permute-start | bytes 1769480 | tf_op jit(solution)/shard_map/ppermute | solution.py:21
  99.7 6.2 %collective-permute-start.4 = (f32[3,2,2,128]{3,2,1,0:T(2,128)S(1)}, f32[3,2,2,128]{3,2,1,0:T(2,128)S(1)}, u32[]{:S(2)}, u32[]{:S(2)}) collective-permute-start(f32[3,2,2,128]{3,2,1,0:T(2,128)S(1)} %get-tuple-element.129), channel_id=1, source_target_pairs={{1,0},{2,1},{3,2},{4,3},{5,4},{6,5},{7,6},{9,8},{10,9},{11,10},{12... | collective-permute-start | bytes 18440 | tf_op jit(solution)/shard_map/ppermute | solution.py:23
  103.1 5.5 %collective-permute-start.5 = (f32[3,2,2,128]{3,2,1,0:T(2,128)S(1)}, f32[3,2,2,128]{3,2,1,0:T(2,128)S(1)}, u32[]{:S(2)}, u32[]{:S(2)}) collective-permute-start(f32[3,2,2,128]{3,2,1,0:T(2,128)S(1)} %get-tuple-element.128), channel_id=1, source_target_pairs={{0,1},{1,2},{2,3},{3,4},{4,5},{5,6},{6,7},{8,9},{9,10},{10,11},{11... | collective-permute-start | bytes 18440 | tf_op jit(solution)/shard_map/ppermute | solution.py:21
  111.6 1.3 copy-start.1
  114.8 23.5 %all-to-all-start.3 = ((f32[2,8,96]{2,0,1:T(2,128)}), f32[2,8,96]{2,0,1:T(2,128)S(1)}, u32[]{:S(2)}, u32[]{:S(2)}) async-start(f32[2,8,96]{2,0,1:T(2,128)} %pad_maximum_fusion.13), calls=%async_computation.3 | async-start | bytes 16384 | tf_op jit(solution)/shard_map/all_to_all | solution.py:131
  160.4 13.9 %collective-permute-start.11 = (f32[3,2,192,128]{3,2,1,0:T(8,128)S(1)}, f32[3,2,192,128]{3,2,1,0:T(8,128)S(1)}, u32[]{:S(2)}, u32[]{:S(2)}) collective-permute-start(f32[3,2,192,128]{3,2,1,0:T(8,128)S(1)} %multiply_subtract_fusion.5), channel_id=1, source_target_pairs={{8,0},{16,8},{24,16},{32,24},{40,32},{48,40},{56,48},{64,56},{72,6... | collective-permute-start | bytes 1769480 | tf_op jit(solution)/shard_map/ppermute | solution.py:23
  162.3 14.5 %collective-permute-start.10 = (f32[3,2,192,128]{3,2,1,0:T(8,128)S(1)}, f32[3,2,192,128]{3,2,1,0:T(8,128)S(1)}, u32[]{:S(2)}, u32[]{:S(2)}) collective-permute-start(f32[3,2,192,128]{3,2,1,0:T(8,128)S(1)} %multiply_subtract_fusion.5), channel_id=1, source_target_pairs={{0,8},{8,16},{16,24},{24,32},{32,40},{40,48},{48,56},{56,64},{64,7... | collective-permute-start | bytes 1769480 | tf_op jit(solution)/shard_map/ppermute | solution.py:21
  165.4 6.4 %collective-permute-start.8 = (f32[3,2,2,128]{3,2,1,0:T(2,128)S(1)}, f32[3,2,2,128]{3,2,1,0:T(2,128)S(1)}, u32[]{:S(2)}, u32[]{:S(2)}) collective-permute-start(f32[3,2,2,128]{3,2,1,0:T(2,128)S(1)} %get-tuple-element.113), channel_id=1, source_target_pairs={{1,0},{2,1},{3,2},{4,3},{5,4},{6,5},{7,6},{9,8},{10,9},{11,10},{12... | collective-permute-start | bytes 18440 | tf_op jit(solution)/shard_map/ppermute | solution.py:23
  168.8 5.5 %collective-permute-start.9 = (f32[3,2,2,128]{3,2,1,0:T(2,128)S(1)}, f32[3,2,2,128]{3,2,1,0:T(2,128)S(1)}, u32[]{:S(2)}, u32[]{:S(2)}) collective-permute-start(f32[3,2,2,128]{3,2,1,0:T(2,128)S(1)} %get-tuple-element.112), channel_id=1, source_target_pairs={{0,1},{1,2},{2,3},{3,4},{4,5},{5,6},{6,7},{8,9},{9,10},{10,11},{11... | collective-permute-start | bytes 18440 | tf_op jit(solution)/shard_map/ppermute | solution.py:21
  179.9 23.4 %all-to-all-start.5 = ((f32[2,8,96]{2,0,1:T(2,128)}), f32[2,8,96]{2,0,1:T(2,128)S(1)}, u32[]{:S(2)}, u32[]{:S(2)}) async-start(f32[2,8,96]{2,0,1:T(2,128)} %pad_maximum_fusion.15), calls=%async_computation.5 | async-start | bytes 16384 | tf_op jit(solution)/shard_map/all_to_all | solution.py:131
